TPU v7x, 128 devices: a whole 4x4x4 slice. The times are simulated.
128 devices in a mesh: ctx: 8 (over y, core), tp: 8 (over x_lo, z), pp: 2 (over x_hi).
Axes of the slice: x: 4 (x_hi: 2, x_lo: 2; x = x_hi * 2 + x_lo), y: 4, z: 4, core: 2. Of those that a mesh axis runs over, the one named last changes fastest.
Arguments:
- queries: bfloat16 [2, 2048, 12288], P('pp', 'ctx', 'tp'), may hold values from -8 to 8
- latents: bfloat16 [2, 2048, 576], P('pp', ('ctx', 'tp')), may hold values from -8 to 8
- latent_gain: float32 [2, 512], P('pp'), may hold values from 0.5 to 2
- w_ukv: bfloat16 [2, 512, 16384], P('pp', None, 'tp'), may hold values from -0.25 to 0.25
- w_o: bfloat16 [2, 8192, 7168], P('pp', 'tp'), may hold values from -0.1875 to 0.1875
- residual: bfloat16 [2, 2048, 7168], P('pp', ('ctx', 'tp')), may hold values from -3 to 3
- block_order: int32 [2, 16], P('pp'), may hold values from 0 to 15, each once within a row
Outputs:
- handed: bfloat16 [2, 2048, 7168], P('pp', ('ctx', 'tp'))
Inputs may be any that keep to these rules, and one draw needn't show every extreme that they name: `block_order`: each row names each of the 16 sequence blocks once.
All inputs are finite; a program needn't handle non-finite values.
Results may differ from a plain program's by a relative error of at most 0.02.
Values may be sent and summed in bfloat16 or wider, within the bound.
A program may use at most 128 MiB of HBM per device.

v0:
```python
import jax
import jax.numpy as jnp
from jax import lax
from jax.sharding import PartitionSpec as P

NOPE = 128
ROPE = 64
VDIM = 128
LATENT = 512
score_scale = 0.135


def passed_along(value, axis, steps):
    count = lax.axis_size(axis)
    pairs = [(source, (source + steps) % count) for source in range(count)]
    return lax.ppermute(value, axis, pairs)


def rotate(values, places):
    middle = values.shape[-1] // 2
    freqs = 10000.0 ** (-(jnp.arange(middle).astype(jnp.float32) * 2.0 / values.shape[-1]))
    angles = places[..., None] * freqs
    first_half = values[..., :middle]
    second_half = values[..., middle:]
    return jnp.concatenate(
        [
            first_half * jnp.cos(angles) - second_half * jnp.sin(angles),
            first_half * jnp.sin(angles) + second_half * jnp.cos(angles),
        ],
        axis=-1,
    )


def place_rows(order_row, first, count, block_len):
    row_ids = first + jnp.arange(count, dtype=jnp.int32)
    owners = row_ids // block_len
    table = jnp.arange(order_row.shape[0], dtype=jnp.int32)
    base = jnp.sum(jnp.where(owners[:, None] == table[None, :], order_row[None, :], 0), axis=1)
    return base * block_len + row_ids % block_len


def local(queries, latents, latent_gain, w_ukv, w_o, residual, block_order):
    order_row = block_order[0]
    tp_count = lax.axis_size("tp")
    tok_dev = queries.shape[1]
    block_len = tok_dev // 2
    lat_rows = latents.shape[1]
    heads_here = w_o.shape[1] // VDIM
    query_places = place_rows(order_row, lax.axis_index("ctx") * tok_dev, tok_dev, block_len)
    query_all = queries[0].reshape(tok_dev, heads_here, NOPE + ROPE)
    query_nope = query_all[..., :NOPE]
    query_rope = rotate(
        query_all[..., NOPE:].astype(jnp.float32), query_places.astype(jnp.float32)[:, None]
    ).astype(jnp.bfloat16)
    own_first = (lax.axis_index("ctx") * tp_count + lax.axis_index("tp")) * lat_rows
    own_places = place_rows(order_row, own_first, lat_rows, block_len)
    latent_rows = latents[0].astype(jnp.float32)
    compressed = latent_rows[:, :LATENT]
    scale_rows = lax.rsqrt(jnp.mean(compressed * compressed, axis=-1, keepdims=True) + 1e-06)
    normed = (compressed * scale_rows * latent_gain[0][None, :]).astype(jnp.bfloat16)
    own_rope = rotate(latent_rows[:, LATENT:], own_places.astype(jnp.float32)).astype(jnp.bfloat16)
    own_keys = jnp.concatenate([normed, own_rope], axis=-1)
    up_weights = w_ukv[0]

    def expand(latent_part):
        produced = jnp.dot(latent_part, up_weights, preferred_element_type=jnp.float32).astype(
            jnp.bfloat16
        )
        return produced.reshape(latent_part.shape[0], heads_here, NOPE + VDIM)

    piece = lax.all_gather(own_keys, ("ctx", "tp"), axis=0, tiled=True)
    make_keys = lambda: (expand(piece[:, :LATENT]), piece[:, LATENT:])
    key_places = place_rows(order_row, jnp.int32(0), piece.shape[0], block_len)
    running_max = jnp.full((tok_dev, heads_here), -1e30, jnp.float32)
    key_value, key_rope = make_keys()
    scores = (
        jnp.einsum(
            "thd,nhd->thn", query_nope, key_value[..., :NOPE], preferred_element_type=jnp.float32
        )
        + jnp.einsum("thr,nr->thn", query_rope, key_rope, preferred_element_type=jnp.float32)
    ) * score_scale
    allowed = (key_places[None, :] <= query_places[:, None])[:, None, :]
    scores = jnp.where(allowed, scores, -1e30)
    new_max = jnp.maximum(running_max, jnp.max(scores, axis=-1))
    weights = jnp.where(allowed, jnp.exp(scores - new_max[..., None]), 0.0)
    new_total = jnp.sum(weights, axis=-1)
    new_sum = jnp.einsum(
        "thn,nhd->thd",
        weights.astype(jnp.bfloat16),
        key_value[..., NOPE:],
        preferred_element_type=jnp.float32,
    )
    attention = (
        (new_sum / new_total[..., None]).astype(jnp.bfloat16).reshape(tok_dev, heads_here * VDIM)
    )
    out_weights = w_o[0]
    summed = lax.psum_scatter(
        jnp.dot(attention, out_weights, preferred_element_type=jnp.float32).astype(jnp.bfloat16),
        "tp",
        scatter_dimension=0,
        tiled=True,
    ).astype(jnp.float32)
    mixed = (summed + residual[0].astype(jnp.float32)).astype(jnp.bfloat16)
    handed = passed_along(mixed, "pp", 1)
    return handed[None]


def solution(mesh):
    in_specs = (
        P("pp", "ctx", "tp"),
        P("pp", ("ctx", "tp"), None),
        P("pp", None),
        P("pp", None, "tp"),
        P("pp", "tp", None),
        P("pp", ("ctx", "tp"), None),
        P("pp", None),
    )
    out_specs = P("pp", ("ctx", "tp"), None)
    return jax.shard_map(local, mesh=mesh, in_specs=in_specs, out_specs=out_specs, check_vma=False)
```

profile of v0, /device:TPU:0, one launch (start us, length us, event | category | flops | bytes accessed | tf_op | source)
XLA Modules:
  0.0 292.4 jit_solution(18152602769886171369)
XLA Ops:
  6.5 0.0 copy-start
  6.5 0.0 all-gather.2.cloned.1.call-start
  6.6 0.9 bitcast_convert_fusion
  7.5 0.7 select_reduce_fusion.2
  8.3 0.1 multiply_reduce_fusion
  8.4 0.1 fusion.38
  8.5 0.8 multiply_convert_fusion
  9.3 0.7 pad_maximum_fusion
  10.0 0.0 all-gather.2.cloned.1.call-update
  10.0 0.0 reduce-scatter.2.cloned.1.call-start
  10.1 1.4 copy.26
  11.5 0.0 copy-start.2
  11.5 0.8 select_reduce_fusion.1
  12.3 0.8 select_reduce_fusion
  13.1 0.2 multiply_cosine_fusion
  13.3 0.8 subtract_convert_fusion
  14.1 0.4 broadcast_compare_fusion
  14.5 155.7 %all-gather.2.cloned.1.call-done = bf16[2048,576]{1,0:T(8,128)(2,1)} async-done(((bf16[32,576]{1,0:T(8,128)(2,1)}), bf16[2048,576]{1,0:T(8,128)(2,1)}) %all-gather.2.cloned.1.call-update) | async-done | bytes 2359312 | tf_op jit(solution)/shard_map/all_gather | solution.py:71
  170.2 0.0 copy-done
  170.2 8.3 %convolution_convert_fusion = bf16[2048,2048]{0,1:T(8,128)(2,1)} fusion(bf16[2048,576]{1,0:T(8,128)(2,1)} %all-gather.2.cloned.1.call-done, bf16[1,512,2048]{2,1,0:T(8,128)(2,1)S(1)} %copy-done), kind=kOutput, calls=%fused_computation.13 | convolution fusion | flops 4299161600 | bytes 12582912 | tf_op jit(solution)/shard_map/dot_general | solution.py:66
  178.5 0.0 copy-done.2
  178.5 0.0 copy-start.3
  178.6 0.0 copy-start.4
  178.6 4.7 %fusion.14 = f32[8,2048,256]{2,1,0:T(8,128)S(1)} fusion(bf16[2048,8,256]{0,2,1:T(8,128)(2,1)} %bitcast.39, bf16[256,8,192]{0,2,1:T(8,128)(2,1)} %bitcast.38), kind=kOutput, calls=%fused_computation.14 | convolution fusion | flops 1073741824 | bytes 21495808 | tf_op jit(solution)/shard_map/thd,nhd->thn/dot_general | solution.py:77
  183.3 0.0 copy-done.3
  183.3 0.0 copy-done.4
  183.3 8.8 %fusion.57 = (f32[256,8]{0,1:T(8,128)S(1)}, f32[256,8,2048]{0,2,1:T(8,128)}) fusion(bf16[256,8,32]{0,2,1:T(8,128)(2,1)S(1)} %copy-done.4, bf16[256,8,32]{0,2,1:T(8,128)(2,1)S(1)} %copy-done.3, bf16[2048,576]{1,0:T(8,128)(2,1)} %all-gather.2.cloned.1.call-done, f32[8,2048,256]{2,1,0:T(8,128)S(1)} %fusion.14, pred[256,2048]{0,1:T(8,128)(4,1)S(1)} %broadcast_compare_fusion), kind=kOutput, calls=%fused_computation.89 | convolution fusion | flops 554170368 | bytes 34873344 | tf_op jit(solution)/shard_map/thr,nr->thn/dot_general | solution.py:80
  192.1 8.6 %fusion.4 = f32[256,8]{0,1:T(8,128)S(1)} fusion(f32[256,8,2048]{0,2,1:T(8,128)} %get-tuple-element.14, f32[256,8]{0,1:T(8,128)S(1)} %broadcast_maximum_fusion, pred[256,2048]{0,1:T(8,128)(4,1)S(1)} %broadcast_compare_fusion), kind=kLoop, calls=%fused_computation.6 | loop fusion | flops 12580864 | bytes 17317888 | tf_op jit(solution)/shard_map/reduce_sum | solution.py:86
  200.8 10.1 %divide_convert_fusion = bf16[256,8,128]{0,2,1:T(8,128)(2,1)S(1)} fusion(f32[256,8,2048]{0,2,1:T(8,128)} %get-tuple-element.14, f32[256,8]{0,1:T(8,128)S(1)} %broadcast_maximum_fusion, pred[256,2048]{0,1:T(8,128)(4,1)S(1)} %broadcast_compare_fusion, bf16[2048,8,256]{0,2,1:T(8,128)(2,1)} %bitcast.40, f32[256,8]{0,1:T(8,128)S(1)} %fusion.4), kind=kOutput, calls=%fused_computation.20 | convolution fusion | flops 1086849024 | bytes 22036480 | tf_op jit(solution)/shard_map/thn,nhd->thd/dot_general | solution.py:87
  210.9 0.0 copy-start.1
  210.9 0.0 copy-start.5
  210.9 11.0 %fusion.6 = bf16[256,7168]{1,0:T(8,128)(2,1)} fusion(bf16[256,1024]{0,1:T(8,128)(2,1)S(1)} %bitcast.41, bf16[1,1024,7168]{2,1,0:T(8,128)(2,1)} %param.11), kind=kOutput, calls=%fused_computation.8 | convolution fusion | flops 3759931392 | bytes 18874368 | tf_op jit(solution)/shard_map/dot_general | solution.py:98
  221.8 0.0 reduce-scatter.2.cloned.1.call-update
  221.9 49.7 %reduce-scatter.2.cloned.1.call-done = bf16[32,7168]{1,0:T(8,128)(2,1)} async-done(((bf16[256,7168]{1,0:T(8,128)(2,1)}), bf16[32,7168]{1,0:T(8,128)(2,1)}) %reduce-scatter.2.cloned.1.call-update) | async-done | bytes 458768 | tf_op jit(solution)/shard_map/reduce_scatter | solution.py:97
  271.6 0.0 copy-done.5
  271.6 1.1 fusion.28
  272.7 2.7 collective-permute-start
  275.4 9.4 %collective-permute-done = bf16[32,7168]{1,0:T(8,128)(2,1)S(1)} collective-permute-done((bf16[32,7168]{1,0:T(8,128)(2,1)S(1)}, bf16[32,7168]{1,0:T(8,128)(2,1)S(1)}, u32[]{:S(2)}, u32[]{:S(2)}) %collective-permute-start) | collective-permute-done | bytes 458784 | tf_op jit(solution)/shard_map/ppermute | solution.py:16
  284.8 0.8 copy.37
  285.6 0.0 copy-done.1
  (10 shorter events, 0.1 us)
Async XLA Ops:
  6.5 163.7 %copy-start = (bf16[1,512,2048]{2,1,0:T(8,128)(2,1)S(1)}, bf16[1,512,2048]{2,1,0:T(8,128)(2,1)}, u32[]{:S(2)}) copy-start(bf16[1,512,2048]{2,1,0:T(8,128)(2,1)} %param.10) | copy-start | bytes 6291460
  6.5 163.7 %all-gather.2.cloned.1.call-start = ((), (), s32[]{:S(2)}) async-start(), calls=%async_computation.1 | async-start | bytes 2662400 | tf_op jit(solution)/shard_map/all_gather | solution.py:71
  10.0 261.6 %reduce-scatter.2.cloned.1.call-start = ((), (), s32[]{:S(2)}) async-start(), calls=%async_computation.2 | async-start | bytes 4128768 | tf_op jit(solution)/shard_map/reduce_scatter | solution.py:97
  11.5 167.1 %copy-start.2 = (bf16[1,256,1536]{1,2,0:T(8,128)(2,1)}, bf16[1,256,1536]{1,2,0:T(8,128)(2,1)S(1)}, u32[]{:S(2)}) copy-start(bf16[1,256,1536]{1,2,0:T(8,128)(2,1)S(1)} %copy.26) | copy-start | bytes 2359300
  178.5 4.7 %copy-start.3 = (bf16[256,8,32]{0,2,1:T(8,128)(2,1)S(1)}, bf16[256,8,32]{0,2,1:T(8,128)(2,1)}, u32[]{:S(2)}) copy-start(bf16[256,8,32]{0,2,1:T(8,128)(2,1)} %get-tuple-element.7) | copy-start | bytes 393220
  178.6 4.7 %copy-start.4 = (bf16[256,8,32]{0,2,1:T(8,128)(2,1)S(1)}, bf16[256,8,32]{0,2,1:T(8,128)(2,1)}, u32[]{:S(2)}) copy-start(bf16[256,8,32]{0,2,1:T(8,128)(2,1)} %get-tuple-element.8) | copy-start | bytes 393220
  210.9 74.7 %copy-start.1 = (bf16[1,512,2048]{2,1,0:T(8,128)(2,1)S(1)}, bf16[1,512,2048]{2,1,0:T(8,128)(2,1)}, u32[]{:S(2)}) copy-start(bf16[1,512,2048]{2,1,0:T(8,128)(2,1)} %param.10) | copy-start | bytes 6291460
  210.9 60.7 %copy-start.5 = (bf16[1,32,7168]{2,1,0:T(8,128)(2,1)S(1)}, bf16[1,32,7168]{2,1,0:T(8,128)(2,1)}, u32[]{:S(2)}) copy-start(bf16[1,32,7168]{2,1,0:T(8,128)(2,1)} %param.12) | copy-start | bytes 1376260
  272.7 12.1 %collective-permute-start = (bf16[32,7168]{1,0:T(8,128)(2,1)S(1)}, bf16[32,7168]{1,0:T(8,128)(2,1)S(1)}, u32[]{:S(2)}, u32[]{:S(2)}) collective-permute-start(bf16[32,7168]{1,0:T(8,128)(2,1)S(1)} %fusion.28), channel_id=1, source_target_pairs={{0,1},{1,0},{2,3},{3,2},{4,5},{5,4},{6,7},{7,6},{8,9},{9,8},{10,11... | collective-permute-start | bytes 1376264 | tf_op jit(solution)/shard_map/ppermute | solution.py:16
Sparse Core Ops, SparseCore 0:
  10.1 160.0 all-gather.1
  222.0 49.5 reduce-scatter.1
where the time goes:
time: 293 us; the launch traced here: 292 us
  waiting for transfers between devices  215 us (73%)
  matrix products  42.9 us (15%)
  other arithmetic  16.2 us (6%)
  between operations  13.5 us (5%)
    all_gather x1, waiting for transfers between devices, local(): piece = lax.all_gather(own_keys, ('ctx', 'tp'), axis=0, tiled=True)  156 us
    reduce_scatter x1, waiting for transfers between devices, local(): lax.psum_scatter(jnp.dot(attention, out_weights, preferred_element_type=j...  49.7 us
    dot_general x1, matrix products, local(): jnp.dot(attention, out_weights, preferred_element_type=jnp.float32)  11 us
    dot_general x1, matrix products, local(): jnp.einsum('thn,nhd->thd', weights.astype(jnp.bfloat16), key_value[..., N...  10.1 us
    ppermute x1, waiting for transfers between devices, passed_along(): return lax.ppermute(value, axis, pairs)  9.41 us
    dot_general x1, matrix products, local(): jnp.einsum('thr,nr->thn', query_rope, key_rope, preferred_element_type=jn...  8.81 us
    reduce_sum x1, other arithmetic, local(): new_total = jnp.sum(weights, axis=-1)  8.63 us
    dot_general x1, matrix products, expand(): jnp.dot(latent_part, up_weights, preferred_element_type=jnp.float32)  8.34 us
  transfers between devices with their start and end apart: 3, of which 3 were waited for; matrix products, arithmetic and copies ran while one was open for 2% of the time, Pallas kernels for 0%

commit v1 on v0

--- a/solution.py
+++ b/solution.py
@@ -68,7 +68,10 @@
         )
         return produced.reshape(latent_part.shape[0], heads_here, NOPE + VDIM)
 
-    piece = lax.all_gather(own_keys, ("ctx", "tp"), axis=0, tiled=True)
+    piece = jnp.concatenate(
+        lax.all_to_all(jnp.stack([own_keys] * lax.axis_size(("ctx", "tp"))), ("ctx", "tp"), 0, 0),
+        axis=0,
+    )
     make_keys = lambda: (expand(piece[:, :LATENT]), piece[:, LATENT:])
     key_places = place_rows(order_row, jnp.int32(0), piece.shape[0], block_len)
     running_max = jnp.full((tok_dev, heads_here), -1e30, jnp.float32)

time: 293 us -> 176 us (0.60)
  waiting for transfers between devices: 215 us -> 87.9 us
  starting transfers between devices: 2.77 us -> 13 us
    all_gather x1 -> x0, waiting for transfers between devices: 156 us -> none  [local(): piece = lax.all_gather(own_keys, ('ctx', 'tp'), axis=0, tiled=True)]
    all_to_all x0 -> x1, waiting for transfers between devices: none -> 30.2 us  [local(): lax.all_to_all(jnp.stack([own_keys] * lax.axis_size(('ctx', 'tp'))), ('ct...]
    all_to_all x0 -> x1, starting transfers between devices: none -> 10.2 us  [local(): lax.all_to_all(jnp.stack([own_keys] * lax.axis_size(('ctx', 'tp'))), ('ct...]
where the time goes in v1:
time: 176 us
  waiting for transfers between devices  87.9 us (50%)
  matrix products  43 us (24%)
  other arithmetic  14.3 us (8%)
  between operations  13.5 us (8%)
  starting transfers between devices  13 us (7%)
  local copies, waits for them, and re-layouts  3.91 us (2%)
    reduce_scatter x1, waiting for transfers between devices, local(): lax.psum_scatter(jnp.dot(attention, out_weights, preferred_element_type=j...  48.3 us
    all_to_all x1, waiting for transfers between devices, local(): lax.all_to_all(jnp.stack([own_keys] * lax.axis_size(('ctx', 'tp'))), ('ct...  30.2 us
    dot_general x1, matrix products, local(): jnp.dot(attention, out_weights, preferred_element_type=jnp.float32)  11 us
    all_to_all x1, starting transfers between devices, local(): lax.all_to_all(jnp.stack([own_keys] * lax.axis_size(('ctx', 'tp'))), ('ct...  10.2 us
    dot_general x1, matrix products, local(): jnp.einsum('thn,nhd->thd', weights.astype(jnp.bfloat16), key_value[..., N...  10.1 us
    ppermute x1, waiting for transfers between devices, passed_along(): return lax.ppermute(value, axis, pairs)  9.34 us
    dot_general x1, matrix products, local(): jnp.einsum('thr,nr->thn', query_rope, key_rope, preferred_element_type=jn...  8.82 us
    reduce_sum x1, other arithmetic, local(): new_total = jnp.sum(weights, axis=-1)  8.63 us
  transfers between devices with their start and end apart: 3, of which 3 were waited for; matrix products, arithmetic and copies ran while one was open for 2% of the time, Pallas kernels for 0%

profile of v1, /device:TPU:0, one launch (start us, length us, event | category | flops | bytes accessed | tf_op | source)
XLA Modules:
  0.0 175.6 jit_solution(10296650977998473844)
XLA Ops:
  6.5 0.0 copy-start
  6.5 0.0 copy-start.6
  6.6 0.9 bitcast_convert_fusion
  7.5 0.7 select_reduce_fusion.2
  8.3 0.1 multiply_reduce_fusion
  8.4 0.1 fusion.38
  8.5 0.8 multiply_convert_fusion
  9.3 0.1 pad_maximum_fusion
  9.4 1.7 stack.2
  11.1 10.2 %all-to-all-start = ((bf16[64,32,576]{2,1,0:T(8,128)(2,1)}), bf16[64,32,576]{2,1,0:T(8,128)(2,1)}, u32[]{:S(2)}, u32[]{:S(2)}) async-start(bf16[64,32,576]{2,1,0:T(8,128)(2,1)} %stack.2), calls=%async_computation | async-start | bytes 5242880 | tf_op jit(solution)/shard_map/all_to_all | solution.py:72
  21.3 0.0 reduce-scatter.2.cloned.1.call-start
  21.3 1.4 copy.20
  22.7 0.0 copy-start.2
  22.8 0.0 copy-done.6
  22.8 0.1 select_reduce_fusion.1
  22.9 0.1 select_reduce_fusion
  23.0 0.2 multiply_cosine_fusion
  23.3 0.8 subtract_convert_fusion
  24.0 0.4 broadcast_compare_fusion
  24.5 30.2 %all-to-all-done = bf16[64,32,576]{2,1,0:T(8,128)(2,1)} async-done(((bf16[64,32,576]{2,1,0:T(8,128)(2,1)}), bf16[64,32,576]{2,1,0:T(8,128)(2,1)}, u32[]{:S(2)}, u32[]{:S(2)}) %all-to-all-start) | async-done | bytes 2359328 | tf_op jit(solution)/shard_map/all_to_all | solution.py:72
  54.7 0.0 copy-done
  54.7 8.3 %convolution_convert_fusion = bf16[2048,2048]{0,1:T(8,128)(2,1)} fusion(bf16[2048,576]{1,0:T(8,128)(2,1)} %bitcast.4, bf16[1,512,2048]{2,1,0:T(8,128)(2,1)S(1)} %copy-done), kind=kOutput, calls=%fused_computation.13 | convolution fusion | flops 4299161600 | bytes 12582912 | tf_op jit(solution)/shard_map/dot_general | solution.py:66
  63.1 0.0 copy-done.2
  63.1 0.0 copy-start.3
  63.1 0.0 copy-start.4
  63.1 4.7 %fusion.14 = f32[8,2048,256]{2,1,0:T(8,128)S(1)} fusion(bf16[2048,8,256]{0,2,1:T(8,128)(2,1)} %bitcast.40, bf16[256,8,192]{0,2,1:T(8,128)(2,1)} %bitcast.39), kind=kOutput, calls=%fused_computation.14 | convolution fusion | flops 1073741824 | bytes 21495808 | tf_op jit(solution)/shard_map/thd,nhd->thn/dot_general | solution.py:80
  67.8 0.0 copy-done.3
  67.8 0.0 copy-done.4
  67.8 8.8 %fusion.57 = (f32[256,8]{0,1:T(8,128)S(1)}, f32[256,8,2048]{0,2,1:T(8,128)}) fusion(bf16[256,8,32]{0,2,1:T(8,128)(2,1)S(1)} %copy-done.4, bf16[256,8,32]{0,2,1:T(8,128)(2,1)S(1)} %copy-done.3, bf16[2048,576]{1,0:T(8,128)(2,1)} %bitcast.4, f32[8,2048,256]{2,1,0:T(8,128)S(1)} %fusion.14, pred[256,2048]{0,1:T(8,128)(4,1)S(1)} %broadcast_compare_fusion), kind=kOutput, calls=%fused_computation.89 | convolution fusion | flops 554170368 | bytes 34873344 | tf_op jit(solution)/shard_map/thr,nr->thn/dot_general | solution.py:83
  76.7 8.6 %fusion.4 = f32[256,8]{0,1:T(8,128)S(1)} fusion(f32[256,8,2048]{0,2,1:T(8,128)} %get-tuple-element.14, f32[256,8]{0,1:T(8,128)S(1)} %broadcast_maximum_fusion, pred[256,2048]{0,1:T(8,128)(4,1)S(1)} %broadcast_compare_fusion), kind=kLoop, calls=%fused_computation.6 | loop fusion | flops 12580864 | bytes 17317888 | tf_op jit(solution)/shard_map/reduce_sum | solution.py:89
  85.3 10.1 %divide_convert_fusion = bf16[256,8,128]{0,2,1:T(8,128)(2,1)S(1)} fusion(f32[256,8,2048]{0,2,1:T(8,128)} %get-tuple-element.14, f32[256,8]{0,1:T(8,128)S(1)} %broadcast_maximum_fusion, pred[256,2048]{0,1:T(8,128)(4,1)S(1)} %broadcast_compare_fusion, bf16[2048,8,256]{0,2,1:T(8,128)(2,1)} %bitcast.41, f32[256,8]{0,1:T(8,128)S(1)} %fusion.4), kind=kOutput, calls=%fused_computation.20 | convolution fusion | flops 1086849024 | bytes 22036480 | tf_op jit(solution)/shard_map/thn,nhd->thd/dot_general | solution.py:90
  95.4 0.0 copy-start.1
  95.4 0.0 copy-start.5
  95.4 11.0 %fusion.6 = bf16[256,7168]{1,0:T(8,128)(2,1)} fusion(bf16[256,1024]{0,1:T(8,128)(2,1)S(1)} %bitcast.42, bf16[1,1024,7168]{2,1,0:T(8,128)(2,1)} %param.11), kind=kOutput, calls=%fused_computation.8 | convolution fusion | flops 3759931392 | bytes 18874368 | tf_op jit(solution)/shard_map/dot_general | solution.py:101
  106.4 0.0 reduce-scatter.2.cloned.1.call-update
  106.4 48.3 %reduce-scatter.2.cloned.1.call-done = bf16[32,7168]{1,0:T(8,128)(2,1)} async-done(((bf16[256,7168]{1,0:T(8,128)(2,1)}), bf16[32,7168]{1,0:T(8,128)(2,1)}) %reduce-scatter.2.cloned.1.call-update) | async-done | bytes 458768 | tf_op jit(solution)/shard_map/reduce_scatter | solution.py:100
  154.7 0.0 copy-done.5
  154.7 1.1 fusion.28
  155.8 2.7 %collective-permute-start = (bf16[32,7168]{1,0:T(8,128)(2,1)S(1)}, bf16[32,7168]{1,0:T(8,128)(2,1)S(1)}, u32[]{:S(2)}, u32[]{:S(2)}) collective-permute-start(bf16[32,7168]{1,0:T(8,128)(2,1)S(1)} %fusion.28), channel_id=1, source_target_pairs={{0,1},{1,0},{2,3},{3,2},{4,5},{5,4},{6,7},{7,6},{8,9},{9,8},{10,11... | collective-permute-start | bytes 1376264 | tf_op jit(solution)/shard_map/ppermute | solution.py:16
  158.6 9.3 %collective-permute-done = bf16[32,7168]{1,0:T(8,128)(2,1)S(1)} collective-permute-done((bf16[32,7168]{1,0:T(8,128)(2,1)S(1)}, bf16[32,7168]{1,0:T(8,128)(2,1)S(1)}, u32[]{:S(2)}, u32[]{:S(2)}) %collective-permute-start) | collective-permute-done | bytes 458784 | tf_op jit(solution)/shard_map/ppermute | solution.py:16
  167.9 0.8 copy.31
  168.7 0.0 copy-done.1
  (10 shorter events, 0.1 us)
Async XLA Ops:
  6.5 48.2 %copy-start = (bf16[1,512,2048]{2,1,0:T(8,128)(2,1)S(1)}, bf16[1,512,2048]{2,1,0:T(8,128)(2,1)}, u32[]{:S(2)}) copy-start(bf16[1,512,2048]{2,1,0:T(8,128)(2,1)} %param.10) | copy-start | bytes 6291460
  6.5 16.2 %copy-start.6 = (s32[1,16]{1,0:T(1,128)S(1)}, s32[1,16]{1,0:T(1,128)}, u32[]{:S(2)}) copy-start(s32[1,16]{1,0:T(1,128)} %param.13) | copy-start | bytes 196
  11.1 43.6 %all-to-all-start = ((bf16[64,32,576]{2,1,0:T(8,128)(2,1)}), bf16[64,32,576]{2,1,0:T(8,128)(2,1)}, u32[]{:S(2)}, u32[]{:S(2)}) async-start(bf16[64,32,576]{2,1,0:T(8,128)(2,1)} %stack.2), calls=%async_computation | async-start | bytes 5242880 | tf_op jit(solution)/shard_map/all_to_all | solution.py:72
  21.3 133.4 %reduce-scatter.2.cloned.1.call-start = ((), (), s32[]{:S(2)}) async-start(), calls=%async_computation.2 | async-start | bytes 4128768 | tf_op jit(solution)/shard_map/reduce_scatter | solution.py:100
  22.7 40.3 %copy-start.2 = (bf16[1,256,1536]{1,2,0:T(8,128)(2,1)}, bf16[1,256,1536]{1,2,0:T(8,128)(2,1)S(1)}, u32[]{:S(2)}) copy-start(bf16[1,256,1536]{1,2,0:T(8,128)(2,1)S(1)} %copy.20) | copy-start | bytes 2359300
  63.1 4.7 %copy-start.3 = (bf16[256,8,32]{0,2,1:T(8,128)(2,1)S(1)}, bf16[256,8,32]{0,2,1:T(8,128)(2,1)}, u32[]{:S(2)}) copy-start(bf16[256,8,32]{0,2,1:T(8,128)(2,1)} %get-tuple-element.7) | copy-start | bytes 393220
  63.1 4.7 %copy-start.4 = (bf16[256,8,32]{0,2,1:T(8,128)(2,1)S(1)}, bf16[256,8,32]{0,2,1:T(8,128)(2,1)}, u32[]{:S(2)}) copy-start(bf16[256,8,32]{0,2,1:T(8,128)(2,1)} %get-tuple-element.8) | copy-start | bytes 393220
  95.4 73.3 %copy-start.1 = (bf16[1,512,2048]{2,1,0:T(8,128)(2,1)S(1)}, bf16[1,512,2048]{2,1,0:T(8,128)(2,1)}, u32[]{:S(2)}) copy-start(bf16[1,512,2048]{2,1,0:T(8,128)(2,1)} %param.10) | copy-start | bytes 6291460
  95.4 59.3 %copy-start.5 = (bf16[1,32,7168]{2,1,0:T(8,128)(2,1)S(1)}, bf16[1,32,7168]{2,1,0:T(8,128)(2,1)}, u32[]{:S(2)}) copy-start(bf16[1,32,7168]{2,1,0:T(8,128)(2,1)} %param.12) | copy-start | bytes 1376260
  155.8 12.1 %collective-permute-start = (bf16[32,7168]{1,0:T(8,128)(2,1)S(1)}, bf16[32,7168]{1,0:T(8,128)(2,1)S(1)}, u32[]{:S(2)}, u32[]{:S(2)}) collective-permute-start(bf16[32,7168]{1,0:T(8,128)(2,1)S(1)} %fusion.28), channel_id=1, source_target_pairs={{0,1},{1,0},{2,3},{3,2},{4,5},{5,4},{6,7},{7,6},{8,9},{9,8},{10,11... | collective-permute-start | bytes 1376264 | tf_op jit(solution)/shard_map/ppermute | solution.py:16
Sparse Core Ops, SparseCore 0:
  106.5 48.1 reduce-scatter.1
